TPU v7x, 512 devices: a whole 4x4x16 slice. The times are simulated.
512 devices in a mesh: section: 8 (over z_hi, core), ctx: 64 (over x, y, z_lo).
Axes of the slice: x: 4, y: 4, z: 16 (z_hi: 4, z_lo: 4; z = z_hi * 4 + z_lo), core: 2. Of those that a mesh axis runs over, the one named last changes fastest.
Arguments:
- down_queries: bfloat16 [8, 8192, 2304], P('section', 'ctx'), may hold values from -40 to 40
- down_keys: bfloat16 [8, 8192, 2304], P('section', 'ctx'), may hold values from -40 to 40
- down_values: bfloat16 [8, 8192, 2304], P('section', 'ctx'), may hold values from -6 to 6
- up_queries: bfloat16 [8, 8192, 2304], P('section', 'ctx'), may hold values from -40 to 40
- up_keys: bfloat16 [8, 8192, 2304], P('section', 'ctx'), may hold values from -40 to 40
- up_values: bfloat16 [8, 8192, 2304], P('section', 'ctx'), may hold values from -6 to 6
- key_blocks: int32 [64, 2], P('ctx'), may hold values from -1 to 47, as said below
Outputs:
- forward: bfloat16 [8, 8192, 2304], P('section', 'ctx')
- handed: bfloat16 [8, 8192, 2304], P('section', 'ctx')
Inputs may be any that keep to these rules, and one draw needn't show every extreme that they name: `key_blocks`: slot k (counting from 1) of query block i holds i - k * 16 or -1, and -1 wherever i - k * 16 is negative.
All inputs are finite; a program needn't handle non-finite values.
Results may differ from a plain program's by a relative error of at most 0.0038.
Values may be sent and summed in bfloat16 or wider, within the bound.
A program may use at most 64 MiB of HBM per device.

v0:
```python
import math

import jax
import jax.numpy as jnp
from jax import lax
from jax.sharding import PartitionSpec as P

HEAD_DIM = 64
BLOCK = 128


def shifted(block, axis, distance):
    devices = range(lax.axis_size(axis))
    route = [(i - distance, i) for i in devices if i - distance in devices]
    return lax.ppermute(block, axis, route)


def on_device(down_queries, down_keys, down_values, up_queries, up_keys, up_values, key_blocks):
    queries = jnp.concatenate([down_queries, up_queries], 0)
    key_values = jnp.stack(
        [jnp.concatenate([down_keys, down_values], 0), jnp.concatenate([up_keys, up_values], 0)]
    )
    tok_rows = queries.shape[1]
    width = queries.shape[2]
    blocks_dev = key_blocks.shape[0]
    strided_count = key_blocks.shape[1]
    head_count = width // HEAD_DIM
    spacing = lax.axis_size("ctx") // 4
    far_pairs = []
    for offset_step in range(1, strided_count + 1):
        far_pairs.append(shifted(key_values, "ctx", offset_step * spacing))
    present = key_blocks >= 0
    causal = jnp.arange(BLOCK)[:, None] >= jnp.arange(BLOCK)[None, :]
    allowed_parts = [causal[None, None]]
    for offset_step in range(strided_count):
        allowed_parts.append(
            jnp.broadcast_to(
                present[:, offset_step][:, None, None, None], (blocks_dev, 1, BLOCK, BLOCK)
            )
        )
    allowed_all = jnp.concatenate(allowed_parts, 3)
    block_shape = (blocks_dev, BLOCK, head_count, HEAD_DIM)
    scale = 1.0 / math.sqrt(HEAD_DIM)
    results = []
    for group_side in range(2):
        query_rows = queries[group_side].reshape(block_shape)
        key_all = jnp.concatenate(
            [key_values[group_side, 0].reshape(block_shape)]
            + [pair_rows[group_side, 0].reshape(block_shape) for pair_rows in far_pairs],
            1,
        )
        value_all = jnp.concatenate(
            [key_values[group_side, 1].reshape(block_shape)]
            + [pair_rows[group_side, 1].reshape(block_shape) for pair_rows in far_pairs],
            1,
        )
        scores = (
            jnp.einsum("nqhd,nkhd->nhqk", query_rows, key_all, preferred_element_type=jnp.float32)
            * scale
        )
        scores = jnp.where(allowed_all, scores, -1e30)
        highest = jnp.max(scores, -1, keepdims=True)
        expo = jnp.exp(scores - highest)
        weights = (expo / jnp.sum(expo, -1, keepdims=True)).astype(jnp.bfloat16)
        mixture = jnp.einsum(
            "nhqk,nkhd->nqhd", weights, value_all, preferred_element_type=jnp.float32
        )
        results.append(mixture.reshape(tok_rows, width).astype(jnp.bfloat16)[None])
    lowered = results[0]
    raised = results[1]
    section_index = lax.axis_index("section")
    last_section = lax.axis_size("section") - 1
    forward = shifted(lowered, "section", 1)
    forward = jnp.where(section_index == 0, raised, forward)
    handed = shifted(raised, "section", -1)
    handed = jnp.where(section_index == last_section, lowered, handed)
    return (forward, handed)


def solution(mesh):
    placed = (
        P("section", "ctx", None),
        P("section", "ctx", None),
        P("section", "ctx", None),
        P("section", "ctx", None),
        P("section", "ctx", None),
        P("section", "ctx", None),
        P("ctx", None),
    )
    return jax.shard_map(
        on_device,
        mesh=mesh,
        in_specs=placed,
        out_specs=(P("section", "ctx", None), P("section", "ctx", None)),
        check_vma=False,
    )
```

profile of v0, /device:TPU:412, one launch (start us, length us, event | category | flops | bytes accessed | tf_op | source)
XLA Modules:
  0.0 184.3 jit_solution(4495037578320180819)
XLA Ops:
  0.6 1.8 maximum_bitcast_fusion.12
  2.5 1.6 pad_maximum_fusion
  4.1 3.2 %collective-permute-start = (bf16[2,2,128,2304]{3,2,1,0:T(8,128)(2,1)}, bf16[2,2,128,2304]{3,2,1,0:T(8,128)(2,1)}, u32[]{:S(2)}, u32[]{:S(2)}) collective-permute-start(bf16[2,2,128,2304]{3,2,1,0:T(8,128)(2,1)} %pad_maximum_fusion), channel_id=1, source_target_pairs={{0,16},{1,17},{2,18},{3,19},{4,20},{5,21},{6,22},{7,23},{8,24},{9,... | collective-permute-start | bytes 7077896 | tf_op jit(solution)/shard_map/ppermute | solution.py:15
  7.3 1.3 collective-permute-start.1
  10.6 0.7 broadcast_in_dim.44
  11.3 1.1 copy.37
  12.7 1.4 copy.35
  14.1 1.1 copy.29
  15.2 0.8 add_bitcast_fusion
  16.0 44.6 %collective-permute-done = bf16[2,2,128,2304]{3,2,1,0:T(8,128)(2,1)} collective-permute-done((bf16[2,2,128,2304]{3,2,1,0:T(8,128)(2,1)}, bf16[2,2,128,2304]{3,2,1,0:T(8,128)(2,1)}, u32[]{:S(2)}, u32[]{:S(2)}) %collective-permute-start) | collective-permute-done | bytes 2359328 | tf_op jit(solution)/shard_map/ppermute | solution.py:15
  60.5 2.8 %fusion.40 = (bf16[1,1,128,2304]{3,2,1,0:T(8,128)(2,1)}, bf16[1,1,128,2304]{3,2,1,0:T(8,128)(2,1)S(1)}, bf16[1,1,128,2304]{3,2,1,0:T(8,128)(2,1)}, bf16[1,1,128,2304]{3,2,1,0:T(8,128)(2,1)S(1)}) fusion(bf16[2,2,128,2304]{3,2,1,0:T(8,128)(2,1)} %collective-permute-done), kind=kLoop, calls=%fused_computation.58 | loop fusion | bytes 4718592 | tf_op jit(solution)/shard_map/slice | solution.py:54
  63.3 1.1 copy.41
  64.3 45.6 %collective-permute-done.1 = bf16[2,2,128,2304]{3,2,1,0:T(8,128)(2,1)} collective-permute-done((bf16[2,2,128,2304]{3,2,1,0:T(8,128)(2,1)}, bf16[2,2,128,2304]{3,2,1,0:T(8,128)(2,1)}, u32[]{:S(2)}, u32[]{:S(2)}) %collective-permute-start.1) | collective-permute-done | bytes 2359328 | tf_op jit(solution)/shard_map/ppermute | solution.py:15
  109.9 2.9 %fusion.41 = (bf16[1,1,128,2304]{3,2,1,0:T(8,128)(2,1)}, bf16[1,1,128,2304]{3,2,1,0:T(8,128)(2,1)}, bf16[1,1,128,2304]{3,2,1,0:T(8,128)(2,1)}, bf16[1,1,128,2304]{3,2,1,0:T(8,128)(2,1)S(1)}) fusion(bf16[2,2,128,2304]{3,2,1,0:T(8,128)(2,1)} %collective-permute-done.1), kind=kLoop, calls=%fused_computation.59 | loop fusion | bytes 4718592 | tf_op jit(solution)/shard_map/slice | solution.py:54
  112.8 2.1 %copy.42 = bf16[1,1,128,2304]{2,3,1,0:T(8,128)(2,1)} copy(bf16[1,1,128,2304]{3,2,1,0:T(8,128)(2,1)} %get-tuple-element.7) | data formatting | bytes 1179648 | tf_op jit(solution)/shard_map/slice | solution.py:49
  115.0 2.1 %copy.38 = bf16[1,1,128,2304]{2,3,1,0:T(8,128)(2,1)} copy(bf16[1,1,128,2304]{3,2,1,0:T(8,128)(2,1)} %get-tuple-element.2) | data formatting | bytes 1179648 | tf_op jit(solution)/shard_map/slice | solution.py:54
  117.1 2.1 %copy.39 = bf16[1,1,128,2304]{2,3,1,0:T(8,128)(2,1)} copy(bf16[1,1,128,2304]{3,2,1,0:T(8,128)(2,1)} %get-tuple-element.6) | data formatting | bytes 1179648 | tf_op jit(solution)/shard_map/slice | solution.py:54
  119.2 2.1 %copy.33 = bf16[1,1,128,2304]{2,3,1,0:T(8,128)(2,1)} copy(bf16[1,1,128,2304]{3,2,1,0:T(8,128)(2,1)} %get-tuple-element.4) | data formatting | bytes 1179648 | tf_op jit(solution)/shard_map/slice | solution.py:49
  121.3 2.1 %copy.34 = bf16[1,1,128,2304]{2,3,1,0:T(8,128)(2,1)} copy(bf16[1,1,128,2304]{3,2,1,0:T(8,128)(2,1)} %get-tuple-element.8) | data formatting | bytes 1179648 | tf_op jit(solution)/shard_map/slice | solution.py:49
  123.5 2.4 %fusion.25 = f32[36,384,128]{2,1,0:T(8,128)S(1)} fusion(bf16[128,36,64]{0,2,1:T(8,128)(2,1)S(1)} %bitcast.73, bf16[1,128,36,64]{1,3,2,0:T(8,128)(2,1)} %bitcast.79, bf16[1,128,36,64]{1,3,2,0:T(8,128)(2,1)} %bitcast.76, bf16[1,128,36,64]{1,3,2,0:T(8,128)(2,1)S(1)} %bitcast.72), kind=kOutput, calls=%fused_computation.36 | convolution fusion | flops 231800832 | bytes 9437184 | tf_op jit(solution)/shard_map/nqhd,nkhd->nhqk/dot_general | solution.py:58
  125.9 4.5 %fusion.46 = (f32[36,128]{1,0:T(8,128)}, f32[36,128,384]{1,2,0:T(8,128)}) fusion(f32[36,384,128]{2,1,0:T(8,128)S(1)} %fusion.25, pred[128,384]{0,1:T(8,128)(4,1)S(1)} %copy-done.7), kind=kOutput, calls=%fused_computation.64 | output fusion | flops 10617215 | bytes 14223360 | tf_op jit(solution)/shard_map/sub | solution.py:63
  130.4 1.1 fusion.16
  131.5 4.5 %fusion.45 = (f32[36,128]{1,0:T(8,128)}, f32[36,128,384]{1,2,0:T(8,128)}) fusion(f32[36,384,128]{2,1,0:T(8,128)S(1)} %fusion.16, pred[128,384]{0,1:T(8,128)(4,1)S(1)} %copy-done.7), kind=kOutput, calls=%fused_computation.63 | output fusion | flops 10617215 | bytes 14223360 | tf_op jit(solution)/shard_map/sub | solution.py:63
  136.1 1.1 copy.30
  137.4 4.0 %fusion.31 = bf16[36,64,128]{2,1,0:T(8,128)(2,1)S(1)} fusion(f32[36,128,384]{1,2,0:T(8,128)} %get-tuple-element.17, f32[36,128]{1,0:T(8,128)} %get-tuple-element.16, bf16[1,128,36,64]{1,3,2,0:T(8,128)(2,1)S(1)} %bitcast.85, bf16[1,128,36,64]{1,3,2,0:T(8,128)(2,1)} %bitcast.84, bf16[1,128,36,64]{1,3,2,0:T(8,128)(2,1)S(1)} %bitcast.81), kind=kOutput, calls=%fused_computation.42 | convolution fusion | flops 235634688 | bytes 9455616 | tf_op jit(solution)/shard_map/nhqk,nkhd->nqhd/dot_general | solution.py:65
  141.7 4.0 %collective-permute-start.3 = (bf16[1,128,2304]{2,1,0:T(8,128)(2,1)S(1)}, bf16[1,128,2304]{2,1,0:T(8,128)(2,1)S(1)}, u32[]{:S(2)}, u32[]{:S(2)}) collective-permute-start(bf16[1,128,2304]{2,1,0:T(8,128)(2,1)S(1)} %copy.46), channel_id=1, source_target_pairs={{64,0},{128,64},{192,128},{256,192},{320,256},{384,320},{448,384},... | collective-permute-start | bytes 1769480 | tf_op jit(solution)/shard_map/ppermute | solution.py:15
  145.7 3.8 %fusion.30 = bf16[36,64,128]{2,1,0:T(8,128)(2,1)S(1)} fusion(f32[36,128,384]{1,2,0:T(8,128)} %get-tuple-element.19, f32[36,128]{1,0:T(8,128)} %get-tuple-element.18, bf16[1,128,36,64]{1,3,2,0:T(8,128)(2,1)S(1)} %bitcast.83, bf16[1,128,36,64]{1,3,2,0:T(8,128)(2,1)S(1)} %bitcast.82, bf16[1,128,36,64]{1,3,2,0:T(8,128)(2,1)S(1)} %bitcast.80), kind=kOutput, calls=%fused_computation.41 | convolution fusion | flops 235634688 | bytes 9455616 | tf_op jit(solution)/shard_map/nhqk,nkhd->nqhd/dot_general | solution.py:65
  149.8 1.9 %collective-permute-start.2 = (bf16[1,128,2304]{2,1,0:T(8,128)(2,1)S(1)}, bf16[1,128,2304]{2,1,0:T(8,128)(2,1)S(1)}, u32[]{:S(2)}, u32[]{:S(2)}) collective-permute-start(bf16[1,128,2304]{2,1,0:T(8,128)(2,1)S(1)} %copy.45), channel_id=1, source_target_pairs={{0,64},{64,128},{128,192},{192,256},{256,320},{320,384},{384,448},... | collective-permute-start | bytes 1769480 | tf_op jit(solution)/shard_map/ppermute | solution.py:15
  151.7 20.3 %collective-permute-done.3 = bf16[1,128,2304]{2,1,0:T(8,128)(2,1)S(1)} collective-permute-done((bf16[1,128,2304]{2,1,0:T(8,128)(2,1)S(1)}, bf16[1,128,2304]{2,1,0:T(8,128)(2,1)S(1)}, u32[]{:S(2)}, u32[]{:S(2)}) %collective-permute-start.3) | collective-permute-done | bytes 589856 | tf_op jit(solution)/shard_map/ppermute | solution.py:15
  172.0 0.9 broadcast_select_fusion
  172.9 10.5 %collective-permute-done.2 = bf16[1,128,2304]{2,1,0:T(8,128)(2,1)S(1)} collective-permute-done((bf16[1,128,2304]{2,1,0:T(8,128)(2,1)S(1)}, bf16[1,128,2304]{2,1,0:T(8,128)(2,1)S(1)}, u32[]{:S(2)}, u32[]{:S(2)}) %collective-permute-start.2) | collective-permute-done | bytes 589856 | tf_op jit(solution)/shard_map/ppermute | solution.py:15
  183.4 0.9 broadcast_select_fusion.1
  (32 shorter events, 3.2 us)
Async XLA Ops:
  2.4 6.6 %copy-start.2 = (bf16[1,128,2304]{2,1,0:T(8,128)(2,1)S(1)}, bf16[1,128,2304]{2,1,0:T(8,128)(2,1)}, u32[]{:S(2)}) copy-start(bf16[1,128,2304]{2,1,0:T(8,128)(2,1)} %param.7) | copy-start | bytes 1769476
  4.1 5.2 %copy-start.8 = (s32[1,2]{1,0:T(1,128)S(1)}, s32[1,2]{1,0:T(1,128)}, u32[]{:S(2)}) copy-start(s32[1,2]{1,0:T(1,128)} %param.13) | copy-start | bytes 28
  4.1 56.5 %collective-permute-start = (bf16[2,2,128,2304]{3,2,1,0:T(8,128)(2,1)}, bf16[2,2,128,2304]{3,2,1,0:T(8,128)(2,1)}, u32[]{:S(2)}, u32[]{:S(2)}) collective-permute-start(bf16[2,2,128,2304]{3,2,1,0:T(8,128)(2,1)} %pad_maximum_fusion), channel_id=1, source_target_pairs={{0,16},{1,17},{2,18},{3,19},{4,20},{5,21},{6,22},{7,23},{8,24},{9,... | collective-permute-start | bytes 7077896 | tf_op jit(solution)/shard_map/ppermute | solution.py:15
  7.3 102.6 %collective-permute-start.1 = (bf16[2,2,128,2304]{3,2,1,0:T(8,128)(2,1)}, bf16[2,2,128,2304]{3,2,1,0:T(8,128)(2,1)}, u32[]{:S(2)}, u32[]{:S(2)}) collective-permute-start(bf16[2,2,128,2304]{3,2,1,0:T(8,128)(2,1)} %pad_maximum_fusion), channel_id=1, source_target_pairs={{0,32},{1,33},{2,34},{3,35},{4,36},{5,37},{6,38},{7,39},{8,40},{9,... | collective-permute-start | bytes 7077896 | tf_op jit(solution)/shard_map/ppermute | solution.py:15
  123.5 2.4 %copy-start.7 = (pred[128,384]{0,1:T(8,128)(4,1)S(1)}, pred[128,384]{0,1:T(8,128)(4,1)}, u32[]{:S(2)}) copy-start(pred[128,384]{0,1:T(8,128)(4,1)} %add_bitcast_fusion) | copy-start | bytes 147460
  125.9 4.5 %copy-start = (bf16[1,1,128,2304]{2,3,1,0:T(8,128)(2,1)S(1)}, bf16[1,1,128,2304]{2,3,1,0:T(8,128)(2,1)}, u32[]{:S(2)}) copy-start(bf16[1,1,128,2304]{2,3,1,0:T(8,128)(2,1)} %copy.33) | copy-start | bytes 1769476
  125.9 4.5 %copy-start.1 = (bf16[1,1,128,2304]{2,3,1,0:T(8,128)(2,1)S(1)}, bf16[1,1,128,2304]{2,3,1,0:T(8,128)(2,1)}, u32[]{:S(2)}) copy-start(bf16[1,1,128,2304]{2,3,1,0:T(8,128)(2,1)} %copy.34) | copy-start | bytes 1769476
  131.5 5.9 %copy-start.4 = (bf16[1,1,128,2304]{2,3,1,0:T(8,128)(2,1)S(1)}, bf16[1,1,128,2304]{2,3,1,0:T(8,128)(2,1)}, u32[]{:S(2)}) copy-start(bf16[1,1,128,2304]{2,3,1,0:T(8,128)(2,1)} %copy.29) | copy-start | bytes 1769476
  137.4 8.3 %copy-start.3 = (bf16[1,1,128,2304]{2,3,1,0:T(8,128)(2,1)S(1)}, bf16[1,1,128,2304]{2,3,1,0:T(8,128)(2,1)}, u32[]{:S(2)}) copy-start(bf16[1,1,128,2304]{2,3,1,0:T(8,128)(2,1)} %copy.37) | copy-start | bytes 1769476
  137.4 8.3 %copy-start.5 = (bf16[1,1,128,2304]{2,3,1,0:T(8,128)(2,1)S(1)}, bf16[1,1,128,2304]{2,3,1,0:T(8,128)(2,1)}, u32[]{:S(2)}) copy-start(bf16[1,1,128,2304]{2,3,1,0:T(8,128)(2,1)} %copy.38) | copy-start | bytes 1769476
  137.4 8.3 %copy-start.6 = (bf16[1,1,128,2304]{2,3,1,0:T(8,128)(2,1)S(1)}, bf16[1,1,128,2304]{2,3,1,0:T(8,128)(2,1)}, u32[]{:S(2)}) copy-start(bf16[1,1,128,2304]{2,3,1,0:T(8,128)(2,1)} %copy.39) | copy-start | bytes 1769476
  141.7 30.4 %collective-permute-start.3 = (bf16[1,128,2304]{2,1,0:T(8,128)(2,1)S(1)}, bf16[1,128,2304]{2,1,0:T(8,128)(2,1)S(1)}, u32[]{:S(2)}, u32[]{:S(2)}) collective-permute-start(bf16[1,128,2304]{2,1,0:T(8,128)(2,1)S(1)} %copy.46), channel_id=1, source_target_pairs={{64,0},{128,64},{192,128},{256,192},{320,256},{384,320},{448,384},... | collective-permute-start | bytes 1769480 | tf_op jit(solution)/shard_map/ppermute | solution.py:15
  149.8 33.6 %collective-permute-start.2 = (bf16[1,128,2304]{2,1,0:T(8,128)(2,1)S(1)}, bf16[1,128,2304]{2,1,0:T(8,128)(2,1)S(1)}, u32[]{:S(2)}, u32[]{:S(2)}) collective-permute-start(bf16[1,128,2304]{2,1,0:T(8,128)(2,1)S(1)} %copy.45), channel_id=1, source_target_pairs={{0,64},{64,128},{128,192},{192,256},{256,320},{320,384},{384,448},... | collective-permute-start | bytes 1769480 | tf_op jit(solution)/shard_map/ppermute | solution.py:15
where the time goes:
time: 185 us; the launch traced here: 184 us
  waiting for transfers between devices  121 us (65%)
  local copies, waits for them, and re-layouts  25.7 us (14%)
  other arithmetic  15 us (8%)
  matrix products  11.3 us (6%)
  starting transfers between devices  10.5 us (6%)
    ppermute x4, waiting for transfers between devices, shifted(): return lax.ppermute(block, axis, route)  121 us
    slice x6, local copies, waits for them, and re-layouts, on_device(): pair_rows[group_side, 1].reshape(block_shape)  11.3 us
    ppermute x4, starting transfers between devices, shifted(): return lax.ppermute(block, axis, route)  10.5 us
    sub x2, other arithmetic, on_device(): expo = jnp.exp(scores - highest)  9.01 us
    dot_general x2, matrix products, on_device(): jnp.einsum('nhqk,nkhd->nqhd', weights, value_all, preferred_element_type=...  7.74 us
    slice x4, local copies, waits for them, and re-layouts, on_device(): pair_rows[group_side, 0].reshape(block_shape)  7.42 us
  transfers between devices with their start and end apart: 4, of which 4 were waited for; matrix products, arithmetic and copies ran while one was open for 9% of the time, Pallas kernels for 0%

commit v1 on v0

v1 whole, which is shorter than its diff:
```python
import math

import jax
import jax.numpy as jnp
from jax import lax
from jax.experimental import pallas as pl
from jax.experimental.pallas import tpu as pltpu
from jax.sharding import PartitionSpec as P

HEAD_DIM = 64
PAIR = 2 * HEAD_DIM
PAIRS = 1
AHEAD = 4
RELAY = 2
LAG = 2
NEG = -1e30
FLOOR = -5e29
RATE = math.log2(math.e) / math.sqrt(HEAD_DIM)
MESH = pl.DeviceIdType.MESH


def kernel(sections, spacing, kb, dq, dk, dv, uq, uk, uv, fwd, hand, own, got, part_in, stat_in,
           part_out, stat_out, final, flag, flag_in, load_sem, data_send, data_recv, part_send,
           part_recv, stat_send, stat_recv, out_send, out_recv, flag_send, flag_recv):
    s = lax.axis_index("section")
    i = lax.axis_index("ctx")
    x = i // spacing
    rest = i - x * spacing
    right = (s, lax.rem(x + 1, 4) * spacing + rest)
    left = (s, lax.rem(x + 3, 4) * spacing + rest)
    below = (lax.max(s - 1, 0), i)
    above = (lax.min(s + 1, sections - 1), i)
    rows = own.shape[1]
    wide = PAIRS * PAIR
    steps = own.shape[2] // wide
    ins = (dq, dk, dv, uq, uk, uv)
    QD, KD, VD, QU, KU, VU = range(6)

    def lanes(c):
        return pl.ds(pl.multiple_of(c * wide, wide), wide)

    def remote(src, dst, send, recv, where):
        return pltpu.make_async_remote_copy(
            src_ref=src, dst_ref=dst, send_sem=send, recv_sem=recv, device_id=where,
            device_id_type=MESH)

    def data(k, c, src, r, where):
        return remote(src.at[:, lanes(c)], got.at[r, :, lanes(c)], data_send.at[k, c],
                      data_recv.at[r, c], where)

    def send_in(k, c, a, r, where):
        data(k, c, ins[a].at[0], r, where).start()

    def send_on(k, c, r0, r, where):
        data(k, c, got.at[r0], r, where).start()

    def wait_data(c, *slots):
        for r in slots:
            data(0, c, got.at[r], r, right).wait_recv()

    def parts(k, c, src, stat, r, where):
        return (remote(src.at[c], part_in.at[r, c], part_send.at[k, c], part_recv.at[r, c], where),
                remote(stat.at[c], stat_in.at[r, c], stat_send.at[k, c], stat_recv.at[r, c], where))

    def send_part(k, c, r, where):
        for copy in parts(k, c, part_out.at[k], stat_out.at[k], r, where):
            copy.start()

    def relay_part(k, c, r0, r, where):
        for copy in parts(k, c, part_in.at[r0], stat_in.at[r0], r, where):
            copy.start()

    def wait_part(c, *slots):
        for r in slots:
            for copy in parts(0, c, part_in.at[r], stat_in.at[r], r, right):
                copy.wait_recv()

    def out_remote(g, c):
        src = final.at[g, :, lanes(c)]
        dst = (fwd, hand)[g].at[0, :, lanes(c)]
        return remote(src, dst, out_send.at[g, c], out_recv.at[g, c], (above, below)[g])

    def out_local(g, c):
        dst = (hand, fwd)[g].at[0, :, lanes(c)]
        return pltpu.make_async_copy(final.at[g, :, lanes(c)], dst, out_send.at[g, c])

    def ends(g):
        return s == (sections - 1, 0)[g]

    def send_out(g, c):
        @pl.when(ends(g))
        def _():
            out_local(g, c).start()

        @pl.when(jnp.logical_not(ends(g)))
        def _():
            out_remote(g, c).start()

    lane = lax.broadcasted_iota(jnp.int32, (rows, PAIR), 1)
    row = lax.broadcasted_iota(jnp.int32, (PAIR, rows), 0)
    first = row < HEAD_DIM
    key = lax.broadcasted_iota(jnp.int32, (rows, 2 * rows), 0)
    query = lax.broadcasted_iota(jnp.int32, (rows, 2 * rows), 1)
    causal = key <= lax.rem(query, rows)

    def piece(ref, c, p):
        return ref[:, pl.ds(pl.multiple_of(c * wide + p * PAIR, PAIR), PAIR)]

    def spread(v):
        return jnp.where(first, v[:, :rows], v[:, rows:])

    def attend(q, sources):
        zero = jnp.zeros_like(q)
        both = jnp.concatenate([jnp.where(lane < HEAD_DIM, q, zero), jnp.where(lane < HEAD_DIM, zero, q)], 0)
        tops, scores, floored = [], [], True
        for k, v, bias, masked in sources:
            sc = lax.dot_general(k, both, (((1,), (1,)), ((), ())), preferred_element_type=jnp.float32)
            if masked:
                sc = jnp.where(causal, sc, NEG)
            top = jnp.max(sc, 0, keepdims=True)
            if bias is None:
                floored = False
            else:
                top = top + bias
            tops.append(top)
            scores.append(sc)
        high = tops[0]
        for top in tops[1:]:
            high = jnp.maximum(high, top)
        if floored:
            high = jnp.maximum(high, FLOOR)
        total, mixed = None, None
        for (k, v, bias, masked), sc in zip(sources, scores):
            base = high if bias is None else high - bias
            e = jnp.exp2((sc - base) * RATE)
            t = jnp.sum(e, 0, keepdims=True)
            o = lax.dot_general(v, e.astype(jnp.bfloat16), (((0,), (0,)), ((), ())),
                                preferred_element_type=jnp.float32)
            total = t if total is None else total + t
            mixed = o if mixed is None else mixed + o
        return jnp.where(first, mixed[:, :rows], mixed[:, rows:]), high, total

    def merge(items, floored=False):
        high = items[0][1]
        for item in items[1:]:
            high = jnp.maximum(high, item[1])
        if floored:
            high = jnp.maximum(high, FLOOR)
        mixed, total = None, None
        for o, top, t in items:
            w = jnp.exp2((top - high) * RATE)
            mixed = o * spread(w) if mixed is None else mixed + o * spread(w)
            total = t * w if total is None else total + t * w
        return mixed, high, total

    def keep(k, c, p, item):
        o, top, t = item
        part_out[k, c, pl.ds(p * PAIR, PAIR), :] = o.astype(jnp.bfloat16)
        at = 4 * p
        stat_out[k, c, pl.ds(at, 1), :] = top[:, :rows]
        stat_out[k, c, pl.ds(at + 1, 1), :] = top[:, rows:]
        stat_out[k, c, pl.ds(at + 2, 1), :] = t[:, :rows]
        stat_out[k, c, pl.ds(at + 3, 1), :] = t[:, rows:]

    def arrived(r, c, p, bias=None):
        o = part_in[r, c, pl.ds(p * PAIR, PAIR), :].astype(jnp.float32)
        at = 4 * p
        lines = [stat_in[r, c, pl.ds(at + n, 1), :] for n in range(4)]
        top = jnp.concatenate(lines[:2], 1)
        if bias is not None:
            top = top + bias
        return o, top, jnp.concatenate(lines[2:], 1)

    def finish(g, c, p, item):
        o, top, t = item
        o = o * spread(1.0 / t)
        final[g, :, pl.ds(pl.multiple_of(c * wide + p * PAIR, PAIR), PAIR)] = o.T.astype(jnp.bfloat16)

    def mine(a, c, p):
        return piece(own.at[a], c, p)

    def sent(r, c, p):
        return piece(got.at[r], c, p)

    def self_part(g, c, p):
        q, k, v = (mine(3 * g + n, c, p) for n in range(3))
        return attend(q, [(k, v, None, True)])

    def own_bias(slot):
        return flag[pl.ds(slot, 1), :]

    def far_bias(slot):
        return flag_in[pl.ds(slot, 1), :]

    loads = [pltpu.make_async_copy(ins[a].at[0], own.at[a], load_sem.at[a]) for a in range(6)]
    for copy in loads:
        copy.start()
    bias = [jnp.where(kb[0, n] >= 0, 0.0, NEG) for n in range(2)]
    flag_row = lax.broadcasted_iota(jnp.int32, flag.shape, 0)
    flag[...] = jnp.where(flag_row == 0, bias[0], bias[1])

    barrier = pltpu.get_barrier_semaphore()
    for where in (left, right):
        pl.semaphore_signal(barrier, inc=1, device_id=where, device_id_type=MESH)

    @pl.when(s > 0)
    def _():
        pl.semaphore_signal(barrier, inc=1, device_id=below, device_id_type=MESH)

    @pl.when(s < sections - 1)
    def _():
        pl.semaphore_signal(barrier, inc=1, device_id=above, device_id_type=MESH)

    edges = jnp.where(s > 0, 1, 0) + jnp.where(s < sections - 1, 1, 0)
    pl.semaphore_wait(barrier, 2 + edges)

    def flags(k, src, where):
        return remote(src, flag_in, flag_send.at[k], flag_recv.at[0], where)

    def wait_loads():
        for copy in loads:
            copy.wait()

    def ahead(send):
        def go(c, carry):
            send(c)
            return carry

        lax.fori_loop(0, min(AHEAD, steps), go, 0)

    def run(extra, body):
        def go(t, carry):
            body(t)
            return carry

        lax.fori_loop(0, steps + extra, go, 0)

    def when_chunk(c, act):
        @pl.when(jnp.logical_and(c >= 0, c < steps))
        def _():
            act(c)

    def settle(n_data, n_part):
        def go(c, carry):
            for k in range(n_data):
                data(k, c, got.at[0], 0, right).wait_send()
            for k in range(n_part):
                for copy in parts(k, c, part_out.at[k], stat_out.at[k], 0, right):
                    copy.wait_send()
            return carry

        lax.fori_loop(0, steps, go, 0)

    @pl.when(x == 0)
    def _():
        def send(c):
            send_in(0, c, KD, 0, right)
            send_in(1, c, VD, 1, right)

        ahead(send)
        wait_loads()
        flags(0, flag, right).wait_recv()

        def hub(c):
            for p in range(PAIRS):
                finish(0, c, p, self_part(0, c, p))
                finish(1, c, p, self_part(1, c, p))
            wait_data(c, 0, 1, 2, 3, 4)
            for p in range(PAIRS):
                k0, v0 = mine(KU, c, p), mine(VU, c, p)
                k1, v1 = sent(0, c, p), sent(1, c, p)
                keep(1, c, p, attend(sent(3, c, p), [(k1, v1, far_bias(0), False), (k0, v0, far_bias(1), False)]))
                keep(2, c, p, attend(sent(4, c, p), [(k1, v1, None, False)]))
                keep(0, c, p, attend(sent(2, c, p), [(k0, v0, None, False)]))
            send_out(0, c)
            send_out(1, c)
            send_part(1, c, 3, left)
            send_part(2, c, 2, left)
            send_part(0, c, 0, right)

        def body(t):
            when_chunk(t + AHEAD, send)
            hub(t)

        run(0, body)
        settle(2, 3)

    @pl.when(x == 1)
    def _():
        def send(c):
            send_in(0, c, KU, 0, left)
            send_in(1, c, VU, 1, left)
            send_in(2, c, QU, 2, left)

        ahead(send)
        wait_loads()
        flags(0, flag, right).wait_recv()

        def hub(c):
            wait_data(c, 0, 1, 2, 3)
            for p in range(PAIRS):
                k1, v1 = mine(KD, c, p), mine(VD, c, p)
                k0, v0 = sent(0, c, p), sent(1, c, p)
                keep(1, c, p, attend(sent(3, c, p), [(k1, v1, None, False)]))
                keep(0, c, p, attend(sent(2, c, p), [(k1, v1, far_bias(0), False), (k0, v0, far_bias(1), False)]))
                finish(0, c, p, attend(mine(QD, c, p), [(k1, v1, None, True), (k0, v0, own_bias(0), False)]))
            send_part(1, c, 1, right)
            send_part(0, c, 0, right)
            send_out(0, c)

        def close(c):
            wait_part(c, 0)
            for p in range(PAIRS):
                finish(1, c, p, merge([self_part(1, c, p), arrived(0, c, p, own_bias(0))]))
            send_out(1, c)

        def body(t):
            when_chunk(t + AHEAD, send)
            when_chunk(t, hub)
            when_chunk(t - LAG, close)

        run(LAG, body)
        settle(3, 2)

    @pl.when(x == 2)
    def _():
        flags(0, flag, left).start()
        flags(1, flag, right).start()

        def send(c):
            send_in(0, c, QD, 2, left)
            send_in(1, c, QU, 0, right)

        ahead(send)

        def relay(c):
            wait_data(c, 0)
            send_on(2, c, 0, 3, left)

        for c in range(min(RELAY, steps)):
            relay(c)
        wait_loads()
        flags(0, flag, right).wait_recv()

        def side(c):
            wait_data(c, 1)
            for p in range(PAIRS):
                keep(1, c, p, attend(sent(1, c, p), [(mine(KU, c, p), mine(VU, c, p), None, False)]))
            send_part(1, c, 1, right)

        def middle(c):
            wait_part(c, 0, 1)
            for p in range(PAIRS):
                near = attend(sent(0, c, p), [(mine(KD, c, p), mine(VD, c, p), far_bias(0), False)])
                keep(0, c, p, merge([near, arrived(1, c, p, far_bias(1))], True))
                finish(0, c, p, merge([self_part(0, c, p), arrived(0, c, p)]))
            send_part(0, c, 0, right)
            send_out(0, c)

        def close(c):
            wait_part(c, 2)
            for p in range(PAIRS):
                finish(1, c, p, merge([self_part(1, c, p), arrived(2, c, p)]))
            send_out(1, c)

        def body(t):
            when_chunk(t + AHEAD, send)
            when_chunk(t + RELAY, relay)
            when_chunk(t, side)
            when_chunk(t - LAG, middle)
            when_chunk(t - 2 * LAG, close)

        run(2 * LAG, body)
        settle(3, 2)
        for k in range(2):
            flags(k, flag, right).wait_send()

    @pl.when(x == 3)
    def _():
        flags(0, flag, left).start()

        def send(c):
            send_in(0, c, QD, 0, left)
            send_in(1, c, QU, 1, left)
            send_in(2, c, QU, 4, right)

        ahead(send)
        flags(0, flag, right).wait_recv()
        flags(1, flag_in, right).start()

        def relay(c):
            wait_data(c, 0)
            send_on(3, c, 0, 3, right)

        for c in range(min(RELAY, steps)):
            relay(c)
        wait_loads()

        def middle(c):
            wait_part(c, 3)
            relay_part(0, c, 3, 2, left)
            wait_part(c, 1, 2)
            for p in range(PAIRS):
                items = [self_part(1, c, p), arrived(1, c, p, own_bias(0)), arrived(2, c, p, own_bias(1))]
                finish(1, c, p, merge(items))
            send_out(1, c)

        def close(c):
            wait_part(c, 0)
            for p in range(PAIRS):
                finish(0, c, p, merge([self_part(0, c, p), arrived(0, c, p)]))
            send_out(0, c)

        def body(t):
            when_chunk(t + AHEAD, send)
            when_chunk(t + RELAY, relay)
            when_chunk(t - LAG, middle)
            when_chunk(t - 2 * LAG, close)

        run(2 * LAG, body)
        settle(4, 1)
        for k in range(2):
            flags(k, flag, right).wait_send()

    for g in range(2):
        def done(c, carry, g=g):
            @pl.when(ends(g))
            def _():
                out_local(g, c).wait()

            @pl.when(jnp.logical_not(ends(g)))
            def _():
                out_remote(g, c).wait_send()

            @pl.when(jnp.logical_not(ends(1 - g)))
            def _():
                out_remote(g, c).wait_recv()

            return carry

        lax.fori_loop(0, steps, done, 0)


def solution(mesh):
    sections, spacing = mesh.shape["section"], mesh.shape["ctx"] // 4

    def on_device(dq, dk, dv, uq, uk, uv, key_blocks):
        _, rows, width = dq.shape
        wide = PAIRS * PAIR
        steps = width // wide
        half, full = jnp.bfloat16, jnp.float32
        dma = pltpu.SemaphoreType.DMA
        whole = pl.BlockSpec(memory_space=pl.ANY)
        out = jax.ShapeDtypeStruct(dq.shape, half)

        def body(*refs):
            kernel(sections, spacing, *refs)

        return pl.pallas_call(
            body,
            out_shape=(out, out),
            in_specs=[pl.BlockSpec(memory_space=pltpu.SMEM)] + [whole] * 6,
            out_specs=(whole, whole),
            scratch_shapes=[
                pltpu.VMEM((6, rows, width), half),
                pltpu.VMEM((5, rows, width), half),
                pltpu.VMEM((4, steps, wide, rows), half),
                pltpu.VMEM((4, steps, 8, rows), full),
                pltpu.VMEM((3, steps, wide, rows), half),
                pltpu.VMEM((3, steps, 8, rows), full),
                pltpu.VMEM((2, rows, width), half),
                pltpu.VMEM((8, 2 * rows), full),
                pltpu.VMEM((8, 2 * rows), full),
                dma((6,)),
                dma((4, steps)),
                dma((5, steps)),
                dma((3, steps)),
                dma((4, steps)),
                dma((3, steps)),
                dma((4, steps)),
                dma((2, steps)),
                dma((2, steps)),
                dma((2,)),
                dma((1,)),
            ],
            compiler_params=pltpu.CompilerParams(
                collective_id=0, has_side_effects=True, vmem_limit_bytes=40 * 1024 * 1024),
        )(key_blocks, dq, dk, dv, uq, uk, uv)

    placed = (P("section", "ctx", None),) * 6 + (P("ctx", None),)
    return jax.shard_map(
        on_device,
        mesh=mesh,
        in_specs=placed,
        out_specs=(P("section", "ctx", None), P("section", "ctx", None)),
        check_vma=False,
    )
```

time: 185 us -> 76.7 us (0.41)
  the two profiles are of different devices: /device:TPU:412 before, /device:TPU:165 now
where the time goes in v1:
time: 76.7 us; the launch traced here: 76.3 us
  Pallas kernels  67 us (87%)
  local copies, waits for them, and re-layouts  8.66 us (11%)
    pallas_call x1, Pallas kernels, on_device(): pl.pallas_call(body, out_shape=(out, out), in_specs=[pl.BlockSpec(memory_...  67 us
    unnamed x16, local copies, waits for them, and re-layouts  8.66 us

profile of v1, /device:TPU:165, one launch (start us, length us, event | category | flops | bytes accessed | tf_op | source)
XLA Modules:
  0.0 76.3 jit_solution(16945199848575206504)
XLA Ops:
  0.6 0.0 copy-start
  0.6 1.1 %copy-done = bf16[1,128,2304]{2,1,0:T(8,128)(2,1)S(1)} copy-done((bf16[1,128,2304]{2,1,0:T(8,128)(2,1)S(1)}, bf16[1,128,2304]{2,1,0:T(8,128)(2,1)}, u32[]{:S(2)}) %copy-start) | copy-done | bytes 589848
  1.7 0.0 copy-start.1
  1.7 1.1 %copy-done.1 = bf16[1,128,2304]{2,1,0:T(8,128)(2,1)S(1)} copy-done((bf16[1,128,2304]{2,1,0:T(8,128)(2,1)S(1)}, bf16[1,128,2304]{2,1,0:T(8,128)(2,1)}, u32[]{:S(2)}) %copy-start.1) | copy-done | bytes 589848
  2.8 0.0 copy-start.2
  2.8 1.1 %copy-done.2 = bf16[1,128,2304]{2,1,0:T(8,128)(2,1)S(1)} copy-done((bf16[1,128,2304]{2,1,0:T(8,128)(2,1)S(1)}, bf16[1,128,2304]{2,1,0:T(8,128)(2,1)}, u32[]{:S(2)}) %copy-start.2) | copy-done | bytes 589848
  3.8 0.0 copy-start.3
  3.8 1.1 %copy-done.3 = bf16[1,128,2304]{2,1,0:T(8,128)(2,1)S(1)} copy-done((bf16[1,128,2304]{2,1,0:T(8,128)(2,1)S(1)}, bf16[1,128,2304]{2,1,0:T(8,128)(2,1)}, u32[]{:S(2)}) %copy-start.3) | copy-done | bytes 589848
  4.9 0.0 copy-start.4
  4.9 1.1 %copy-done.4 = bf16[1,128,2304]{2,1,0:T(8,128)(2,1)S(1)} copy-done((bf16[1,128,2304]{2,1,0:T(8,128)(2,1)S(1)}, bf16[1,128,2304]{2,1,0:T(8,128)(2,1)}, u32[]{:S(2)}) %copy-start.4) | copy-done | bytes 589848
  6.0 0.0 copy-start.5
  6.0 1.1 %copy-done.5 = bf16[1,128,2304]{2,1,0:T(8,128)(2,1)S(1)} copy-done((bf16[1,128,2304]{2,1,0:T(8,128)(2,1)S(1)}, bf16[1,128,2304]{2,1,0:T(8,128)(2,1)}, u32[]{:S(2)}) %copy-start.5) | copy-done | bytes 589848
  7.0 0.0 copy-start.6
  7.0 0.7 copy-done.6
  7.7 67.0 %shard_map.86 = (bf16[1,128,2304]{2,1,0:T(8,128)(2,1)S(1)}, bf16[1,128,2304]{2,1,0:T(8,128)(2,1)S(1)}) custom-call(s32[1,2]{1,0:T(1,128)S(1)} %copy-done.6, bf16[1,128,2304]{2,1,0:T(8,128)(2,1)S(1)} %copy-done, bf16[1,128,2304]{2,1,0:T(8,128)(2,1)S(1)} %copy-done.1, bf16[1,128,2304]{2,1,0:T(8,128)(2,1)S(1)} %copy-done.2, ...), custom_call_target="tpu_custom_call" | custom-call | tf_op jit(solution)/shard_map/pallas_call | solution.py:459
  74.7 0.8 %copy.11 = bf16[1,128,2304]{2,1,0:T(8,128)(2,1)} copy(bf16[1,128,2304]{2,1,0:T(8,128)(2,1)S(1)} %get-tuple-element.4) | data formatting | bytes 1179648
  75.5 0.8 %copy.12 = bf16[1,128,2304]{2,1,0:T(8,128)(2,1)} copy(bf16[1,128,2304]{2,1,0:T(8,128)(2,1)S(1)} %get-tuple-element.5) | data formatting | bytes 1179648
Async XLA Ops:
  0.6 1.1 %copy-start = (bf16[1,128,2304]{2,1,0:T(8,128)(2,1)S(1)}, bf16[1,128,2304]{2,1,0:T(8,128)(2,1)}, u32[]{:S(2)}) copy-start(bf16[1,128,2304]{2,1,0:T(8,128)(2,1)} %refs_1_.1) | copy-start | bytes 1769476
  1.7 1.1 %copy-start.1 = (bf16[1,128,2304]{2,1,0:T(8,128)(2,1)S(1)}, bf16[1,128,2304]{2,1,0:T(8,128)(2,1)}, u32[]{:S(2)}) copy-start(bf16[1,128,2304]{2,1,0:T(8,128)(2,1)} %refs_2_.1) | copy-start | bytes 1769476
  2.8 1.1 %copy-start.2 = (bf16[1,128,2304]{2,1,0:T(8,128)(2,1)S(1)}, bf16[1,128,2304]{2,1,0:T(8,128)(2,1)}, u32[]{:S(2)}) copy-start(bf16[1,128,2304]{2,1,0:T(8,128)(2,1)} %refs_3_.1) | copy-start | bytes 1769476
  3.8 1.1 %copy-start.3 = (bf16[1,128,2304]{2,1,0:T(8,128)(2,1)S(1)}, bf16[1,128,2304]{2,1,0:T(8,128)(2,1)}, u32[]{:S(2)}) copy-start(bf16[1,128,2304]{2,1,0:T(8,128)(2,1)} %refs_4_.1) | copy-start | bytes 1769476
  4.9 1.1 %copy-start.4 = (bf16[1,128,2304]{2,1,0:T(8,128)(2,1)S(1)}, bf16[1,128,2304]{2,1,0:T(8,128)(2,1)}, u32[]{:S(2)}) copy-start(bf16[1,128,2304]{2,1,0:T(8,128)(2,1)} %refs_5_.1) | copy-start | bytes 1769476
  6.0 1.1 %copy-start.5 = (bf16[1,128,2304]{2,1,0:T(8,128)(2,1)S(1)}, bf16[1,128,2304]{2,1,0:T(8,128)(2,1)}, u32[]{:S(2)}) copy-start(bf16[1,128,2304]{2,1,0:T(8,128)(2,1)} %refs_6_.1) | copy-start | bytes 1769476
  7.0 0.7 copy-start.6

commit v2 on v1

--- a/solution.py
+++ b/solution.py
@@ -10,8 +10,8 @@
 HEAD_DIM = 64
 PAIR = 2 * HEAD_DIM
 PAIRS = 1
-AHEAD = 4
-RELAY = 2
+AHEAD = 6
+RELAY = 3
 LAG = 2
 NEG = -1e30
 FLOOR = -5e29
@@ -262,21 +262,23 @@
         flags(0, flag, right).wait_recv()
 
         def hub(c):
-            for p in range(PAIRS):
-                finish(0, c, p, self_part(0, c, p))
-                finish(1, c, p, self_part(1, c, p))
             wait_data(c, 0, 1, 2, 3, 4)
             for p in range(PAIRS):
                 k0, v0 = mine(KU, c, p), mine(VU, c, p)
                 k1, v1 = sent(0, c, p), sent(1, c, p)
                 keep(1, c, p, attend(sent(3, c, p), [(k1, v1, far_bias(0), False), (k0, v0, far_bias(1), False)]))
-                keep(2, c, p, attend(sent(4, c, p), [(k1, v1, None, False)]))
-                keep(0, c, p, attend(sent(2, c, p), [(k0, v0, None, False)]))
+            send_part(1, c, 3, left)
+            for p in range(PAIRS):
+                keep(2, c, p, attend(sent(4, c, p), [(sent(0, c, p), sent(1, c, p), None, False)]))
+            send_part(2, c, 2, left)
+            for p in range(PAIRS):
+                keep(0, c, p, attend(sent(2, c, p), [(mine(KU, c, p), mine(VU, c, p), None, False)]))
+            send_part(0, c, 0, right)
+            for p in range(PAIRS):
+                finish(1, c, p, self_part(1, c, p))
+                finish(0, c, p, self_part(0, c, p))
+            send_out(1, c)
             send_out(0, c)
-            send_out(1, c)
-            send_part(1, c, 3, left)
-            send_part(2, c, 2, left)
-            send_part(0, c, 0, right)
 
         def body(t):
             when_chunk(t + AHEAD, send)
@@ -299,19 +301,24 @@
         def hub(c):
             wait_data(c, 0, 1, 2, 3)
             for p in range(PAIRS):
+                keep(1, c, p, attend(sent(3, c, p), [(mine(KD, c, p), mine(VD, c, p), None, False)]))
+            send_part(1, c, 1, right)
+            for p in range(PAIRS):
                 k1, v1 = mine(KD, c, p), mine(VD, c, p)
                 k0, v0 = sent(0, c, p), sent(1, c, p)
-                keep(1, c, p, attend(sent(3, c, p), [(k1, v1, None, False)]))
                 keep(0, c, p, attend(sent(2, c, p), [(k1, v1, far_bias(0), False), (k0, v0, far_bias(1), False)]))
+            send_part(0, c, 0, right)
+            for p in range(PAIRS):
+                k1, v1 = mine(KD, c, p), mine(VD, c, p)
+                k0, v0 = sent(0, c, p), sent(1, c, p)
                 finish(0, c, p, attend(mine(QD, c, p), [(k1, v1, None, True), (k0, v0, own_bias(0), False)]))
-            send_part(1, c, 1, right)
-            send_part(0, c, 0, right)
             send_out(0, c)
 
         def close(c):
+            own_part = [self_part(1, c, p) for p in range(PAIRS)]
             wait_part(c, 0)
             for p in range(PAIRS):
-                finish(1, c, p, merge([self_part(1, c, p), arrived(0, c, p, own_bias(0))]))
+                finish(1, c, p, merge([own_part[p], arrived(0, c, p, own_bias(0))]))
             send_out(1, c)
 
         def body(t):
@@ -349,18 +356,23 @@
             send_part(1, c, 1, right)
 
         def middle(c):
-            wait_part(c, 0, 1)
-            for p in range(PAIRS):
-                near = attend(sent(0, c, p), [(mine(KD, c, p), mine(VD, c, p), far_bias(0), False)])
-                keep(0, c, p, merge([near, arrived(1, c, p, far_bias(1))], True))
-                finish(0, c, p, merge([self_part(0, c, p), arrived(0, c, p)]))
+            near = [attend(sent(0, c, p), [(mine(KD, c, p), mine(VD, c, p), far_bias(0), False)])
+                    for p in range(PAIRS)]
+            wait_part(c, 1)
+            for p in range(PAIRS):
+                keep(0, c, p, merge([near[p], arrived(1, c, p, far_bias(1))], True))
             send_part(0, c, 0, right)
+            own_part = [self_part(0, c, p) for p in range(PAIRS)]
+            wait_part(c, 0)
+            for p in range(PAIRS):
+                finish(0, c, p, merge([own_part[p], arrived(0, c, p)]))
             send_out(0, c)
 
         def close(c):
+            own_part = [self_part(1, c, p) for p in range(PAIRS)]
             wait_part(c, 2)
             for p in range(PAIRS):
-                finish(1, c, p, merge([self_part(1, c, p), arrived(2, c, p)]))
+                finish(1, c, p, merge([own_part[p], arrived(2, c, p)]))
             send_out(1, c)
 
         def body(t):
@@ -399,16 +411,18 @@
         def middle(c):
             wait_part(c, 3)
             relay_part(0, c, 3, 2, left)
+            own_part = [self_part(1, c, p) for p in range(PAIRS)]
             wait_part(c, 1, 2)
             for p in range(PAIRS):
-                items = [self_part(1, c, p), arrived(1, c, p, own_bias(0)), arrived(2, c, p, own_bias(1))]
+                items = [own_part[p], arrived(1, c, p, own_bias(0)), arrived(2, c, p, own_bias(1))]
                 finish(1, c, p, merge(items))
             send_out(1, c)
 
         def close(c):
+            own_part = [self_part(0, c, p) for p in range(PAIRS)]
             wait_part(c, 0)
             for p in range(PAIRS):
-                finish(0, c, p, merge([self_part(0, c, p), arrived(0, c, p)]))
+                finish(0, c, p, merge([own_part[p], arrived(0, c, p)]))
             send_out(0, c)
 
         def body(t):
@@ -465,9 +479,9 @@
                 pltpu.VMEM((6, rows, width), half),
                 pltpu.VMEM((5, rows, width), half),
                 pltpu.VMEM((4, steps, wide, rows), half),
-                pltpu.VMEM((4, steps, 8, rows), full),
+                pltpu.VMEM((4, steps, 4 * PAIRS, rows), full),
                 pltpu.VMEM((3, steps, wide, rows), half),
-                pltpu.VMEM((3, steps, 8, rows), full),
+                pltpu.VMEM((3, steps, 4 * PAIRS, rows), full),
                 pltpu.VMEM((2, rows, width), half),
                 pltpu.VMEM((8, 2 * rows), full),
                 pltpu.VMEM((8, 2 * rows), full),
@@ -484,7 +498,7 @@
                 dma((1,)),
             ],
             compiler_params=pltpu.CompilerParams(
-                collective_id=0, has_side_effects=True, vmem_limit_bytes=40 * 1024 * 1024),
+                collective_id=0, has_side_effects=True, vmem_limit_bytes=67043328),
         )(key_blocks, dq, dk, dv, uq, uk, uv)
 
     placed = (P("section", "ctx", None),) * 6 + (P("ctx", None),)

time: 76.7 us -> 69.9 us (0.911)
  the two profiles are of different devices: /device:TPU:165 before, /device:TPU:157 now
where the time goes in v2:
time: 69.9 us; the launch traced here: 69.7 us
  Pallas kernels  66.3 us (95%)
  local copies, waits for them, and re-layouts  2.8 us (4%)
    pallas_call x1, Pallas kernels, on_device(): pl.pallas_call(body, out_shape=(out, out), in_specs=[pl.BlockSpec(memory_...  66.3 us
    unnamed x4, local copies, waits for them, and re-layouts  2.8 us

profile of v2, /device:TPU:157, one launch (start us, length us, event | category | flops | bytes accessed | tf_op | source)
XLA Modules:
  0.0 69.7 jit_solution(2776557832595459212)
XLA Ops:
  0.6 66.3 %shard_map.86 = (bf16[1,128,2304]{2,1,0:T(8,128)(2,1)}, bf16[1,128,2304]{2,1,0:T(8,128)(2,1)}) custom-call(s32[1,2]{1,0:T(1,128)} %refs_0_.1, bf16[1,128,2304]{2,1,0:T(8,128)(2,1)} %refs_1_.1, bf16[1,128,2304]{2,1,0:T(8,128)(2,1)} %refs_2_.1, bf16[1,128,2304]{2,1,0:T(8,128)(2,1)} %refs_3_.1, bf16[1,128,2304]{2,1,0:T(8,128)(2,1)} %refs_4_.1, ...), custom_call_target="tpu_custom_call" | custom-call | tf_op jit(solution)/shard_map/pallas_call | solution.py:473
  66.9 0.0 copy-start
  66.9 2.0 %copy.11 = bf16[1,128,2304]{2,1,0:T(8,128)(2,1)} copy(bf16[1,128,2304]{2,1,0:T(8,128)(2,1)} %get-tuple-element.4) | data formatting | bytes 1179648
  68.9 0.0 copy-done
  68.9 0.8 %copy.12 = bf16[1,128,2304]{2,1,0:T(8,128)(2,1)} copy(bf16[1,128,2304]{2,1,0:T(8,128)(2,1)S(1)} %copy-done) | data formatting | bytes 1179648
Async XLA Ops:
  66.9 2.0 %copy-start = (bf16[1,128,2304]{2,1,0:T(8,128)(2,1)S(1)}, bf16[1,128,2304]{2,1,0:T(8,128)(2,1)}, u32[]{:S(2)}) copy-start(bf16[1,128,2304]{2,1,0:T(8,128)(2,1)} %get-tuple-element.5) | copy-start | bytes 1769476

commit v3 on v2

--- a/solution.py
+++ b/solution.py
@@ -10,9 +10,11 @@
 HEAD_DIM = 64
 PAIR = 2 * HEAD_DIM
 PAIRS = 1
-AHEAD = 6
-RELAY = 3
-LAG = 2
+AHEAD = 8
+NEAR = 4
+RELAY = 4
+LAG = 3
+SKEW = 6
 NEG = -1e30
 FLOOR = -5e29
 RATE = math.log2(math.e) / math.sqrt(HEAD_DIM)
@@ -221,12 +223,12 @@
         for copy in loads:
             copy.wait()
 
-    def ahead(send):
+    def ahead(send, count=AHEAD):
         def go(c, carry):
             send(c)
             return carry
 
-        lax.fori_loop(0, min(AHEAD, steps), go, 0)
+        lax.fori_loop(0, min(count, steps), go, 0)
 
     def run(extra, body):
         def go(t, carry):
@@ -262,7 +264,7 @@
         flags(0, flag, right).wait_recv()
 
         def hub(c):
-            wait_data(c, 0, 1, 2, 3, 4)
+            wait_data(c, 0, 1, 3, 4)
             for p in range(PAIRS):
                 k0, v0 = mine(KU, c, p), mine(VU, c, p)
                 k1, v1 = sent(0, c, p), sent(1, c, p)
@@ -272,19 +274,23 @@
                 keep(2, c, p, attend(sent(4, c, p), [(sent(0, c, p), sent(1, c, p), None, False)]))
             send_part(2, c, 2, left)
             for p in range(PAIRS):
-                keep(0, c, p, attend(sent(2, c, p), [(mine(KU, c, p), mine(VU, c, p), None, False)]))
-            send_part(0, c, 0, right)
-            for p in range(PAIRS):
                 finish(1, c, p, self_part(1, c, p))
                 finish(0, c, p, self_part(0, c, p))
             send_out(1, c)
             send_out(0, c)
 
+        def near(c):
+            wait_data(c, 2)
+            for p in range(PAIRS):
+                keep(0, c, p, attend(sent(2, c, p), [(mine(KU, c, p), mine(VU, c, p), None, False)]))
+            send_part(0, c, 0, right)
+
         def body(t):
             when_chunk(t + AHEAD, send)
-            hub(t)
-
-        run(0, body)
+            when_chunk(t, hub)
+            when_chunk(t - SKEW, near)
+
+        run(SKEW, body)
         settle(2, 3)
 
     @pl.when(x == 1)
@@ -292,9 +298,12 @@
         def send(c):
             send_in(0, c, KU, 0, left)
             send_in(1, c, VU, 1, left)
+
+        def send_q(c):
             send_in(2, c, QU, 2, left)
 
         ahead(send)
+        ahead(send_q, AHEAD - SKEW)
         wait_loads()
         flags(0, flag, right).wait_recv()
 
@@ -323,10 +332,11 @@
 
         def body(t):
             when_chunk(t + AHEAD, send)
+            when_chunk(t + AHEAD - SKEW, send_q)
             when_chunk(t, hub)
-            when_chunk(t - LAG, close)
-
-        run(LAG, body)
+            when_chunk(t - SKEW - LAG, close)
+
+        run(SKEW + LAG, body)
         settle(3, 2)
 
     @pl.when(x == 2)
@@ -335,10 +345,13 @@
         flags(1, flag, right).start()
 
         def send(c):
+            send_in(1, c, QU, 0, right)
+
+        def send_q(c):
             send_in(0, c, QD, 2, left)
-            send_in(1, c, QU, 0, right)
 
         ahead(send)
+        ahead(send_q, NEAR)
 
         def relay(c):
             wait_data(c, 0)
@@ -377,6 +390,7 @@
 
         def body(t):
             when_chunk(t + AHEAD, send)
+            when_chunk(t + NEAR, send_q)
             when_chunk(t + RELAY, relay)
             when_chunk(t, side)
             when_chunk(t - LAG, middle)
@@ -394,9 +408,12 @@
         def send(c):
             send_in(0, c, QD, 0, left)
             send_in(1, c, QU, 1, left)
+
+        def send_q(c):
             send_in(2, c, QU, 4, right)
 
         ahead(send)
+        ahead(send_q, NEAR)
         flags(0, flag, right).wait_recv()
         flags(1, flag_in, right).start()
 
@@ -427,6 +444,7 @@
 
         def body(t):
             when_chunk(t + AHEAD, send)
+            when_chunk(t + NEAR, send_q)
             when_chunk(t + RELAY, relay)
             when_chunk(t - LAG, middle)
             when_chunk(t - 2 * LAG, close)

time: 69.9 us -> 75.2 us (1.076)
  the two profiles are of different devices: /device:TPU:157 before, /device:TPU:155 now
where the time goes in v3:
time: 75.2 us; the launch traced here: 75.1 us
  Pallas kernels  71.6 us (95%)
  local copies, waits for them, and re-layouts  2.8 us (4%)
    pallas_call x1, Pallas kernels, on_device(): pl.pallas_call(body, out_shape=(out, out), in_specs=[pl.BlockSpec(memory_...  71.6 us
    unnamed x4, local copies, waits for them, and re-layouts  2.8 us

profile of v3, /device:TPU:155, one launch (start us, length us, event | category | flops | bytes accessed | tf_op | source)
XLA Modules:
  0.0 75.1 jit_solution(8396333404098458483)
XLA Ops:
  0.6 71.6 %shard_map.86 = (bf16[1,128,2304]{2,1,0:T(8,128)(2,1)}, bf16[1,128,2304]{2,1,0:T(8,128)(2,1)}) custom-call(s32[1,2]{1,0:T(1,128)} %refs_0_.1, bf16[1,128,2304]{2,1,0:T(8,128)(2,1)} %refs_1_.1, bf16[1,128,2304]{2,1,0:T(8,128)(2,1)} %refs_2_.1, bf16[1,128,2304]{2,1,0:T(8,128)(2,1)} %refs_3_.1, bf16[1,128,2304]{2,1,0:T(8,128)(2,1)} %refs_4_.1, ...), custom_call_target="tpu_custom_call" | custom-call | tf_op jit(solution)/shard_map/pallas_call | solution.py:491
  72.2 0.0 copy-start
  72.3 2.0 %copy.11 = bf16[1,128,2304]{2,1,0:T(8,128)(2,1)} copy(bf16[1,128,2304]{2,1,0:T(8,128)(2,1)} %get-tuple-element.4) | data formatting | bytes 1179648
  74.2 0.0 copy-done
  74.2 0.8 %copy.12 = bf16[1,128,2304]{2,1,0:T(8,128)(2,1)} copy(bf16[1,128,2304]{2,1,0:T(8,128)(2,1)S(1)} %copy-done) | data formatting | bytes 1179648
Async XLA Ops:
  72.2 2.0 %copy-start = (bf16[1,128,2304]{2,1,0:T(8,128)(2,1)S(1)}, bf16[1,128,2304]{2,1,0:T(8,128)(2,1)}, u32[]{:S(2)}) copy-start(bf16[1,128,2304]{2,1,0:T(8,128)(2,1)} %get-tuple-element.5) | copy-start | bytes 1769476

commit v4 on v3

--- a/solution.py
+++ b/solution.py
@@ -10,11 +10,13 @@
 HEAD_DIM = 64
 PAIR = 2 * HEAD_DIM
 PAIRS = 1
-AHEAD = 8
+DEEP = 10
+AHEAD = 6
 NEAR = 4
-RELAY = 4
-LAG = 3
-SKEW = 6
+RAMP = 5
+LAG = 2
+FAR = 5
+SKEW = 2
 NEG = -1e30
 FLOOR = -5e29
 RATE = math.log2(math.e) / math.sqrt(HEAD_DIM)
@@ -242,6 +244,11 @@
         def _():
             act(c)
 
+    def ramp(t, relay):
+        early = jnp.asarray(t < RAMP)
+        when_chunk(jnp.where(early, 2 * t + 2, t + RAMP + 2), relay)
+        when_chunk(jnp.where(early, 2 * t + 3, -1), relay)
+
     def settle(n_data, n_part):
         def go(c, carry):
             for k in range(n_data):
@@ -302,8 +309,11 @@
         def send_q(c):
             send_in(2, c, QU, 2, left)
 
-        ahead(send)
-        ahead(send_q, AHEAD - SKEW)
+        def send_all(c):
+            when_chunk(c, send)
+            when_chunk(c - SKEW, send_q)
+
+        ahead(send_all, DEEP)
         wait_loads()
         flags(0, flag, right).wait_recv()
 
@@ -331,8 +341,7 @@
             send_out(1, c)
 
         def body(t):
-            when_chunk(t + AHEAD, send)
-            when_chunk(t + AHEAD - SKEW, send_q)
+            send_all(t + DEEP)
             when_chunk(t, hub)
             when_chunk(t - SKEW - LAG, close)
 
@@ -350,15 +359,14 @@
         def send_q(c):
             send_in(0, c, QD, 2, left)
 
-        ahead(send)
         ahead(send_q, NEAR)
+        ahead(send, DEEP)
 
         def relay(c):
             wait_data(c, 0)
             send_on(2, c, 0, 3, left)
 
-        for c in range(min(RELAY, steps)):
-            relay(c)
+        ramp(-1, relay)
         wait_loads()
         flags(0, flag, right).wait_recv()
 
@@ -389,14 +397,14 @@
             send_out(1, c)
 
         def body(t):
-            when_chunk(t + AHEAD, send)
+            when_chunk(t + DEEP, send)
             when_chunk(t + NEAR, send_q)
-            when_chunk(t + RELAY, relay)
+            ramp(t, relay)
             when_chunk(t, side)
             when_chunk(t - LAG, middle)
-            when_chunk(t - 2 * LAG, close)
-
-        run(2 * LAG, body)
+            when_chunk(t - FAR, close)
+
+        run(FAR, body)
         settle(3, 2)
         for k in range(2):
             flags(k, flag, right).wait_send()
@@ -407,13 +415,16 @@
 
         def send(c):
             send_in(0, c, QD, 0, left)
+
+        def send_q(c):
             send_in(1, c, QU, 1, left)
-
-        def send_q(c):
             send_in(2, c, QU, 4, right)
 
-        ahead(send)
-        ahead(send_q, NEAR)
+        def first_sends(c):
+            send(c)
+            when_chunk(jnp.where(c < NEAR, c, -1), send_q)
+
+        ahead(first_sends, DEEP)
         flags(0, flag, right).wait_recv()
         flags(1, flag_in, right).start()
 
@@ -421,8 +432,7 @@
             wait_data(c, 0)
             send_on(3, c, 0, 3, right)
 
-        for c in range(min(RELAY, steps)):
-            relay(c)
+        ramp(-1, relay)
         wait_loads()
 
         def middle(c):
@@ -443,13 +453,13 @@
             send_out(0, c)
 
         def body(t):
-            when_chunk(t + AHEAD, send)
+            when_chunk(t + DEEP, send)
             when_chunk(t + NEAR, send_q)
-            when_chunk(t + RELAY, relay)
+            ramp(t, relay)
             when_chunk(t - LAG, middle)
-            when_chunk(t - 2 * LAG, close)
-
-        run(2 * LAG, body)
+            when_chunk(t - FAR, close)
+
+        run(FAR, body)
         settle(4, 1)
         for k in range(2):
             flags(k, flag, right).wait_send()

time: 75.2 us -> 71.7 us (0.953)
  the two profiles are of different devices: /device:TPU:155 before, /device:TPU:157 now
where the time goes in v4:
time: 71.7 us; the launch traced here: 71.5 us
  Pallas kernels  68.1 us (95%)
  local copies, waits for them, and re-layouts  2.8 us (4%)
    pallas_call x1, Pallas kernels, on_device(): pl.pallas_call(body, out_shape=(out, out), in_specs=[pl.BlockSpec(memory_...  68.1 us
    unnamed x4, local copies, waits for them, and re-layouts  2.8 us

profile of v4, /device:TPU:157, one launch (start us, length us, event | category | flops | bytes accessed | tf_op | source)
XLA Modules:
  0.0 71.5 jit_solution(15078053662341794810)
XLA Ops:
  0.6 68.1 %shard_map.86 = (bf16[1,128,2304]{2,1,0:T(8,128)(2,1)}, bf16[1,128,2304]{2,1,0:T(8,128)(2,1)}) custom-call(s32[1,2]{1,0:T(1,128)} %refs_0_.1, bf16[1,128,2304]{2,1,0:T(8,128)(2,1)} %refs_1_.1, bf16[1,128,2304]{2,1,0:T(8,128)(2,1)} %refs_2_.1, bf16[1,128,2304]{2,1,0:T(8,128)(2,1)} %refs_3_.1, bf16[1,128,2304]{2,1,0:T(8,128)(2,1)} %refs_4_.1, ...), custom_call_target="tpu_custom_call" | custom-call | tf_op jit(solution)/shard_map/pallas_call | solution.py:501
  68.7 0.0 copy-start
  68.7 2.0 %copy.11 = bf16[1,128,2304]{2,1,0:T(8,128)(2,1)} copy(bf16[1,128,2304]{2,1,0:T(8,128)(2,1)} %get-tuple-element.4) | data formatting | bytes 1179648
  70.7 0.0 copy-done
  70.7 0.8 %copy.12 = bf16[1,128,2304]{2,1,0:T(8,128)(2,1)} copy(bf16[1,128,2304]{2,1,0:T(8,128)(2,1)S(1)} %copy-done) | data formatting | bytes 1179648
Async XLA Ops:
  68.7 2.0 %copy-start = (bf16[1,128,2304]{2,1,0:T(8,128)(2,1)S(1)}, bf16[1,128,2304]{2,1,0:T(8,128)(2,1)}, u32[]{:S(2)}) copy-start(bf16[1,128,2304]{2,1,0:T(8,128)(2,1)} %get-tuple-element.5) | copy-start | bytes 1769476

commit v5 on v3

--- a/solution.py
+++ b/solution.py
@@ -14,7 +14,7 @@
 NEAR = 4
 RELAY = 4
 LAG = 3
-SKEW = 6
+SKEW = 3
 NEG = -1e30
 FLOOR = -5e29
 RATE = math.log2(math.e) / math.sqrt(HEAD_DIM)
@@ -334,9 +334,9 @@
             when_chunk(t + AHEAD, send)
             when_chunk(t + AHEAD - SKEW, send_q)
             when_chunk(t, hub)
-            when_chunk(t - SKEW - LAG, close)
-
-        run(SKEW + LAG, body)
+            when_chunk(t - SKEW - 2, close)
+
+        run(SKEW + 2, body)
         settle(3, 2)
 
     @pl.when(x == 2)

time: 75.2 us -> 73.7 us (0.980)
  the two profiles are of different devices: /device:TPU:155 before, /device:TPU:147 now
where the time goes in v5:
time: 73.7 us; the launch traced here: 73.5 us
  Pallas kernels  70.1 us (95%)
  local copies, waits for them, and re-layouts  2.8 us (4%)
    pallas_call x1, Pallas kernels, on_device(): pl.pallas_call(body, out_shape=(out, out), in_specs=[pl.BlockSpec(memory_...  70.1 us
    unnamed x4, local copies, waits for them, and re-layouts  2.8 us

profile of v5, /device:TPU:147, one launch (start us, length us, event | category | flops | bytes accessed | tf_op | source)
XLA Modules:
  0.0 73.5 jit_solution(15237574120719479201)
XLA Ops:
  0.6 70.1 %shard_map.86 = (bf16[1,128,2304]{2,1,0:T(8,128)(2,1)}, bf16[1,128,2304]{2,1,0:T(8,128)(2,1)}) custom-call(s32[1,2]{1,0:T(1,128)} %refs_0_.1, bf16[1,128,2304]{2,1,0:T(8,128)(2,1)} %refs_1_.1, bf16[1,128,2304]{2,1,0:T(8,128)(2,1)} %refs_2_.1, bf16[1,128,2304]{2,1,0:T(8,128)(2,1)} %refs_3_.1, bf16[1,128,2304]{2,1,0:T(8,128)(2,1)} %refs_4_.1, ...), custom_call_target="tpu_custom_call" | custom-call | tf_op jit(solution)/shard_map/pallas_call | solution.py:491
  70.7 0.0 copy-start
  70.7 2.0 %copy.11 = bf16[1,128,2304]{2,1,0:T(8,128)(2,1)} copy(bf16[1,128,2304]{2,1,0:T(8,128)(2,1)} %get-tuple-element.4) | data formatting | bytes 1179648
  72.7 0.0 copy-done
  72.7 0.8 %copy.12 = bf16[1,128,2304]{2,1,0:T(8,128)(2,1)} copy(bf16[1,128,2304]{2,1,0:T(8,128)(2,1)S(1)} %copy-done) | data formatting | bytes 1179648
Async XLA Ops:
  70.7 2.0 %copy-start = (bf16[1,128,2304]{2,1,0:T(8,128)(2,1)S(1)}, bf16[1,128,2304]{2,1,0:T(8,128)(2,1)}, u32[]{:S(2)}) copy-start(bf16[1,128,2304]{2,1,0:T(8,128)(2,1)} %get-tuple-element.5) | copy-start | bytes 1769476

commit v6 on v2

--- a/solution.py
+++ b/solution.py
@@ -9,10 +9,10 @@
 
 HEAD_DIM = 64
 PAIR = 2 * HEAD_DIM
-PAIRS = 1
-AHEAD = 6
-RELAY = 3
-LAG = 2
+PAIRS = 2
+AHEAD = 4
+RELAY = 2
+LAG = 1
 NEG = -1e30
 FLOOR = -5e29
 RATE = math.log2(math.e) / math.sqrt(HEAD_DIM)
@@ -465,7 +465,7 @@
         half, full = jnp.bfloat16, jnp.float32
         dma = pltpu.SemaphoreType.DMA
         whole = pl.BlockSpec(memory_space=pl.ANY)
-        out = jax.ShapeDtypeStruct(dq.shape, half)
+        out = pltpu.VMEM(dq.shape, half)
 
         def body(*refs):
             kernel(sections, spacing, *refs)
@@ -498,7 +498,7 @@
                 dma((1,)),
             ],
             compiler_params=pltpu.CompilerParams(
-                collective_id=0, has_side_effects=True, vmem_limit_bytes=67043328),
+                collective_id=0, has_side_effects=True, vmem_limit_bytes=62000000),
         )(key_blocks, dq, dk, dv, uq, uk, uv)
 
     placed = (P("section", "ctx", None),) * 6 + (P("ctx", None),)

time: 69.9 us -> 71.1 us (1.017)
  Pallas kernels: 66.3 us -> 68.6 us
  local copies, waits for them, and re-layouts: 2.8 us -> 1.63 us
    pallas_call x1, Pallas kernels: 66.3 us -> 68.6 us  [on_device(): pl.pallas_call(body, out_shape=(out, out), in_specs=[pl.BlockSpec(memory_...]
    unnamed x4 -> x2, local copies, waits for them, and re-layouts: 2.8 us -> 1.63 us
where the time goes in v6:
time: 71.1 us; the launch traced here: 70.9 us
  Pallas kernels  68.6 us (96%)
  local copies, waits for them, and re-layouts  1.63 us (2%)
    pallas_call x1, Pallas kernels, on_device(): pl.pallas_call(body, out_shape=(out, out), in_specs=[pl.BlockSpec(memory_...  68.6 us
    unnamed x2, local copies, waits for them, and re-layouts  1.63 us

profile of v6, /device:TPU:157, one launch (start us, length us, event | category | flops | bytes accessed | tf_op | source)
XLA Modules:
  0.0 70.9 jit_solution(7822755274536023969)
XLA Ops:
  0.6 68.6 %shard_map.86 = (bf16[1,128,2304]{2,1,0:T(8,128)(2,1)S(1)}, bf16[1,128,2304]{2,1,0:T(8,128)(2,1)S(1)}) custom-call(s32[1,2]{1,0:T(1,128)} %refs_0_.1, bf16[1,128,2304]{2,1,0:T(8,128)(2,1)} %refs_1_.1, bf16[1,128,2304]{2,1,0:T(8,128)(2,1)} %refs_2_.1, bf16[1,128,2304]{2,1,0:T(8,128)(2,1)} %refs_3_.1, bf16[1,128,2304]{2,1,0:T(8,128)(2,1)} %refs_4_.1, ...), custom_call_target="tpu_custom_call" | custom-call | tf_op jit(solution)/shard_map/pallas_call | solution.py:473
  69.3 0.8 %copy.11 = bf16[1,128,2304]{2,1,0:T(8,128)(2,1)} copy(bf16[1,128,2304]{2,1,0:T(8,128)(2,1)S(1)} %get-tuple-element.2) | data formatting | bytes 1179648
  70.1 0.8 %copy.12 = bf16[1,128,2304]{2,1,0:T(8,128)(2,1)} copy(bf16[1,128,2304]{2,1,0:T(8,128)(2,1)S(1)} %get-tuple-element.3) | data formatting | bytes 1179648

commit v7 on v2

--- a/solution.py
+++ b/solution.py
@@ -379,8 +379,8 @@
             when_chunk(t + AHEAD, send)
             when_chunk(t + RELAY, relay)
             when_chunk(t, side)
+            when_chunk(t - 2 * LAG, close)
             when_chunk(t - LAG, middle)
-            when_chunk(t - 2 * LAG, close)
 
         run(2 * LAG, body)
         settle(3, 2)
@@ -465,7 +465,7 @@
         half, full = jnp.bfloat16, jnp.float32
         dma = pltpu.SemaphoreType.DMA
         whole = pl.BlockSpec(memory_space=pl.ANY)
-        out = jax.ShapeDtypeStruct(dq.shape, half)
+        out = pltpu.VMEM(dq.shape, half)
 
         def body(*refs):
             kernel(sections, spacing, *refs)
@@ -498,7 +498,7 @@
                 dma((1,)),
             ],
             compiler_params=pltpu.CompilerParams(
-                collective_id=0, has_side_effects=True, vmem_limit_bytes=67043328),
+                collective_id=0, has_side_effects=True, vmem_limit_bytes=62000000),
         )(key_blocks, dq, dk, dv, uq, uk, uv)
 
     placed = (P("section", "ctx", None),) * 6 + (P("ctx", None),)

time: 69.9 us -> 67.6 us (0.967)
  local copies, waits for them, and re-layouts: 2.8 us -> 1.63 us
  Pallas kernels: 66.3 us -> 65.2 us
    unnamed x4 -> x2, local copies, waits for them, and re-layouts: 2.8 us -> 1.63 us
    pallas_call x1, Pallas kernels: 66.3 us -> 65.2 us  [on_device(): pl.pallas_call(body, out_shape=(out, out), in_specs=[pl.BlockSpec(memory_...]
where the time goes in v7:
time: 67.6 us; the launch traced here: 67.5 us
  Pallas kernels  65.2 us (96%)
  local copies, waits for them, and re-layouts  1.63 us (2%)
    pallas_call x1, Pallas kernels, on_device(): pl.pallas_call(body, out_shape=(out, out), in_specs=[pl.BlockSpec(memory_...  65.2 us
    unnamed x2, local copies, waits for them, and re-layouts  1.63 us

profile of v7, /device:TPU:157, one launch (start us, length us, event | category | flops | bytes accessed | tf_op | source)
XLA Modules:
  0.0 67.5 jit_solution(2156510431250843080)
XLA Ops:
  0.6 65.2 %shard_map.86 = (bf16[1,128,2304]{2,1,0:T(8,128)(2,1)S(1)}, bf16[1,128,2304]{2,1,0:T(8,128)(2,1)S(1)}) custom-call(s32[1,2]{1,0:T(1,128)} %refs_0_.1, bf16[1,128,2304]{2,1,0:T(8,128)(2,1)} %refs_1_.1, bf16[1,128,2304]{2,1,0:T(8,128)(2,1)} %refs_2_.1, bf16[1,128,2304]{2,1,0:T(8,128)(2,1)} %refs_3_.1, bf16[1,128,2304]{2,1,0:T(8,128)(2,1)} %refs_4_.1, ...), custom_call_target="tpu_custom_call" | custom-call | tf_op jit(solution)/shard_map/pallas_call | solution.py:473
  65.8 0.8 %copy.11 = bf16[1,128,2304]{2,1,0:T(8,128)(2,1)} copy(bf16[1,128,2304]{2,1,0:T(8,128)(2,1)S(1)} %get-tuple-element.2) | data formatting | bytes 1179648
  66.7 0.8 %copy.12 = bf16[1,128,2304]{2,1,0:T(8,128)(2,1)} copy(bf16[1,128,2304]{2,1,0:T(8,128)(2,1)S(1)} %get-tuple-element.3) | data formatting | bytes 1179648
